TPU v7x, 32 devices: a whole 2x2x4 slice. The times are simulated.
32 devices in a mesh: long: 8 (over y, x, core), short: 4 (over z).
Axes of the slice: x: 2, y: 2, z: 4, core: 2. Of those that a mesh axis runs over, the one named last changes fastest.
Arguments:
- transition: float32 [64, 384, 384], P(('long', 'short')), may hold values from 0 to 1
- innovation: float32 [64, 384], P(('long', 'short')), may hold values from 20 to 80
- observation: float32 [64, 384], P(('long', 'short')), may hold values from 0.05 to 0.5
- effects: float32 [64, 384, 384], P(('long', 'short')), may hold values from -0.0045 to 0.0045
- prior: float32 [384], replicated, may hold values from 0.5 to 2
- right_side: float32 [64, 384, 128], P(('long', 'short')), may hold values from -3 to 3
- tip_right: float32 [384, 128], replicated, may hold values from -6 to 6
Outputs:
- solution: float32 [64, 384, 128], P(('long', 'short'))
- tip_solution: float32 [384, 128], replicated
All inputs are finite; a program needn't handle non-finite values.
Results may differ from a plain program's by a relative error of at most 0.0003.
Values sent between devices are 32-bit elements; how exact they have to be, the bound alone decides.
A program may use at most 256 MiB of HBM per device.

v0:
```python
import jax
import jax.numpy as jnp
from jax import lax
from jax.experimental import pallas as pl
from jax.experimental.pallas import tpu as pltpu
from jax.sharding import PartitionSpec as P

AXES = ("long", "short")
PREC = lax.Precision.HIGHEST
FAST = lax.Precision.HIGHEST
LANES = 128
SUBLANES = 8


def gram_prod(left, right, precision=FAST):
    return jnp.einsum("ji,jk->ik", left, right, precision=precision)


def mat_prod(left, right, precision=FAST):
    return jnp.matmul(left, right, precision=precision)


def inverse_two(a, b, c):
    inv = 1.0 / (a * c - b * b)
    return c * inv, -(b * inv), a * inv


def pivot_four(tiles, first, lane, sub):
    group, row = divmod(first, SUBLANES)
    shape = (SUBLANES, LANES)
    cols = [
        [jnp.broadcast_to(t[:, first + k : first + k + 1], shape) for t in tiles] for k in range(4)
    ]

    def entry(i, k):
        return cols[k][group][row + i : row + i + 1, :]

    a00, a01, a11 = inverse_two(entry(0, 0), entry(0, 1), entry(1, 1))
    b00, b01, b10, b11 = entry(0, 2), entry(0, 3), entry(1, 2), entry(1, 3)
    m00, m01 = a00 * b00 + a01 * b10, a00 * b01 + a01 * b11
    m10, m11 = a01 * b00 + a11 * b10, a01 * b01 + a11 * b11
    s00, s01, s11 = inverse_two(
        entry(2, 2) - (b00 * m00 + b10 * m10),
        entry(2, 3) - (b00 * m01 + b10 * m11),
        entry(3, 3) - (b01 * m01 + b11 * m11),
    )
    u00, u01 = m00 * s00 + m01 * s01, m00 * s01 + m01 * s11
    u10, u11 = m10 * s00 + m11 * s01, m10 * s01 + m11 * s11
    t01 = a01 + (u00 * m10 + u01 * m11)
    pivot_inverse = (
        (a00 + (u00 * m00 + u01 * m01), t01, -u00, -u01),
        (t01, a11 + (u10 * m10 + u11 * m11), -u10, -u11),
        (-u00, -u10, s00, s01),
        (-u01, -u11, s01, s11),
    )
    inside = jnp.logical_and(lane >= first, lane < first + 4)
    rows = [
        jnp.where(
            inside[:1],
            jnp.where(lane[:1] == first + k, 1.0, 0.0),
            tiles[group][row + k : row + k + 1, :],
        )
        for k in range(4)
    ]
    scaled = [
        jnp.broadcast_to(
            (p[0] * rows[0] + p[1] * rows[1]) + (p[2] * rows[2] + p[3] * rows[3]), shape
        )
        for p in pivot_inverse
    ]
    out = []
    for place, tile in enumerate(tiles):
        new = jnp.where(inside, 0.0, tile)
        for k in range(4):
            new = new - cols[k][place] * scaled[k]
        if place == group:
            for k in range(4):
                new = jnp.where(sub == row + k, scaled[k], new)
        out.append(new)
    return out


def inverse_kernel(a_ref, o_ref):
    width = a_ref.shape[0]
    lane = lax.broadcasted_iota(jnp.int32, (SUBLANES, LANES), 1)
    sub = lax.broadcasted_iota(jnp.int32, (SUBLANES, LANES), 0)
    o_ref[...] = a_ref[...]

    def step(k, carry):
        at = pl.multiple_of(k * LANES, LANES)
        here = pl.ds(at, LANES)
        tiles = [
            o_ref[pl.ds(pl.multiple_of(at + SUBLANES * g, SUBLANES), SUBLANES), here]
            for g in range(LANES // SUBLANES)
        ]
        for first in range(0, LANES, 4):
            tiles = pivot_four(tiles, first, lane, sub)
        pivot = jnp.concatenate(tiles, axis=0)
        rows = o_ref[here, :]
        columns = o_ref[:, here]
        scaled = jnp.dot(pivot, rows, precision=PREC, preferred_element_type=jnp.float32)
        o_ref[here, :] = scaled
        o_ref[here, here] = pivot
        scaled = o_ref[here, :]
        o_ref[:, here] = jnp.zeros((width, LANES), jnp.float32)
        o_ref[...] = o_ref[...] - jnp.dot(
            columns, scaled, precision=PREC, preferred_element_type=jnp.float32
        )
        o_ref[here, :] = scaled
        return carry

    lax.fori_loop(0, width // LANES, step, 0)


def spd_inverse(matrix):
    width = matrix.shape[0]
    return pl.pallas_call(
        inverse_kernel,
        out_shape=jax.ShapeDtypeStruct(matrix.shape, jnp.float32),
        in_specs=[pl.BlockSpec(memory_space=pltpu.VMEM)],
        out_specs=pl.BlockSpec(memory_space=pltpu.VMEM),
        cost_estimate=pl.CostEstimate(
            flops=300 * width**3, bytes_accessed=8 * width**2, transcendentals=0
        ),
        name="spd_inverse",
    )(matrix)


def body(transition, innovation, observation, effects, prior, right_side, tip_right):
    block_count, node_width = innovation.shape
    tip_width = prior.shape[0]
    total = lax.axis_size(AXES)
    position = lax.axis_index(AXES)
    identity = jnp.eye(node_width, dtype=jnp.float32)

    def send(values, pairs):
        return lax.ppermute(values, AXES, pairs)

    weighted_trans = innovation[:, :, None] * transition
    weighted_effect = innovation[:, :, None] * effects
    succ_diag = [gram_prod(transition[t], weighted_trans[t], PREC) for t in range(block_count)]
    succ_arrow = [gram_prod(transition[t], weighted_effect[t], PREC) for t in range(block_count)]
    tip_terms = gram_prod(
        effects.reshape(-1, tip_width), weighted_effect.reshape(-1, tip_width), PREC
    )
    global_block = position * block_count + jnp.arange(block_count)
    couple = -weighted_trans * jnp.where(global_block == 0, 0.0, 1.0)[:, None, None]
    diag_base = (innovation + observation)[:, :, None] * identity
    interior = block_count - 1

    stored = []
    left_diag = left_arrow = left_rhs = 0.0
    diag_item = arrow_item = rhs_item = left_item = None
    for t in range(block_count):
        if t == 0:
            diag_item = diag_base[t]
            arrow_item = -weighted_effect[t]
            rhs_item = right_side[t]
            left_item = couple[t]
        else:
            _, link, y_left, y_arrow, y_rhs = stored[-1]
            diag_item = diag_base[t] - mat_prod(couple[t], link)
            arrow_item = -weighted_effect[t] - mat_prod(couple[t], y_arrow)
            rhs_item = right_side[t] - mat_prod(couple[t], y_rhs)
            left_item = -mat_prod(couple[t], y_left)
        if t < interior:
            diag_item = diag_item + succ_diag[t + 1]
            arrow_item = arrow_item + succ_arrow[t + 1]
            inverse = spd_inverse(diag_item)
            link = jnp.einsum("ij,kj->ik", inverse, couple[t + 1], precision=FAST)
            y_left = mat_prod(inverse, left_item)
            y_arrow = mat_prod(inverse, arrow_item)
            y_rhs = mat_prod(inverse, rhs_item)
            left_diag = left_diag - gram_prod(left_item, y_left)
            left_arrow = left_arrow - gram_prod(left_item, y_arrow)
            left_rhs = left_rhs - gram_prod(left_item, y_rhs)
            tip_terms = tip_terms - gram_prod(arrow_item, y_arrow)
            tip_part = gram_prod(arrow_item, y_rhs)
            tip_rhs_terms = -tip_part if t == 0 else tip_rhs_terms - tip_part
            stored.append((inverse, link, y_left, y_arrow, y_rhs))
    if interior == 0:
        tip_rhs_terms = jnp.zeros_like(tip_right)

    to_left = [(i, i - 1) for i in range(1, total)]
    node_diag = diag_item + send(left_diag + succ_diag[0], to_left)
    node_arrow = arrow_item + send(left_arrow + succ_arrow[0], to_left)
    node_rhs = rhs_item
    if interior > 0:
        node_rhs = node_rhs + send(left_rhs, to_left)
    node_couple = left_item

    levels = []
    distance = 1
    while distance < total:
        d = distance
        drops = [i for i in range(total) if (i + 1) % d == 0 and (i + 1) // d % 2 == 1]
        rightward = [(i, i + d) for i in drops if i + d < total]
        leftward = [(i, i - d) for i in drops if i >= d]
        back_right = [(j, i) for i, j in rightward]
        back_left = [(j, i) for i, j in leftward]
        rank = position + 1
        drop = jnp.logical_and(rank % d == 0, rank // d % 2 == 1)
        fed = jnp.logical_and(rank % (2 * d) == 0, position >= d)
        right_item = send(node_couple, back_right).T
        inverse = spd_inverse(node_diag)
        y_right = mat_prod(inverse, right_item)
        y_left = mat_prod(inverse, node_couple)
        diag_right = send(gram_prod(right_item, y_right), rightward)
        diag_left = send(gram_prod(node_couple, y_left), leftward)
        y_arrow = mat_prod(inverse, node_arrow)
        y_rhs = mat_prod(inverse, node_rhs)
        new_couple = send(gram_prod(right_item, y_left), rightward)
        arrow_right = send(gram_prod(right_item, y_arrow), rightward)
        arrow_left = send(gram_prod(node_couple, y_arrow), leftward)
        rhs_right = send(gram_prod(right_item, y_rhs), rightward)
        rhs_left = send(gram_prod(node_couple, y_rhs), leftward)
        tip_passed = send(tip_terms - gram_prod(node_arrow, y_arrow), rightward)
        tip_rhs_passed = send(tip_rhs_terms - gram_prod(node_arrow, y_rhs), rightward)
        tip_terms = tip_terms + tip_passed
        tip_rhs_terms = tip_rhs_terms + tip_rhs_passed
        levels.append((drop, back_left, back_right, y_left, y_right, y_arrow, y_rhs))
        node_diag = node_diag - diag_right - diag_left
        node_couple = jnp.where(fed, -new_couple, node_couple)
        node_arrow = node_arrow - arrow_right - arrow_left
        node_rhs = node_rhs - rhs_right - rhs_left
        distance *= 2

    final = position == total - 1
    inverse = spd_inverse(node_diag)
    y_arrow = mat_prod(inverse, node_arrow)
    y_rhs = mat_prod(inverse, node_rhs)
    tip_total = tip_terms - gram_prod(node_arrow, y_arrow) + jnp.diag(prior)
    tip_rhs_total = tip_rhs_terms - gram_prod(node_arrow, y_rhs) + tip_right
    tip_found = mat_prod(spd_inverse(tip_total), tip_rhs_total)
    tip_solution = jnp.where(final, tip_found, 0.0)
    node_x = jnp.where(final, y_rhs - mat_prod(y_arrow, tip_solution), 0.0)

    for drop, back_left, back_right, y_left, y_right, y_arrow, y_rhs in reversed(levels):
        tip_solution = tip_solution + send(tip_solution, back_right)
        left_x = send(node_x, back_left)
        right_x = send(node_x, back_right)
        value = (
            y_rhs
            - mat_prod(y_arrow, tip_solution)
            - mat_prod(y_left, left_x)
            - mat_prod(y_right, right_x)
        )
        node_x = jnp.where(drop, value, node_x)
    left_x = send(node_x, [(i, i + 1) for i in range(total - 1)])
    outs = [node_x]
    for inverse, link, y_left, y_arrow, y_rhs in reversed(stored):
        value = (
            y_rhs
            - mat_prod(y_arrow, tip_solution)
            - mat_prod(y_left, left_x)
            - mat_prod(link, outs[0])
        )
        outs.insert(0, value)
    return (jnp.stack(outs, axis=0), tip_solution)


def solution(mesh):
    placed = (
        P(AXES, None, None),
        P(AXES, None),
        P(AXES, None),
        P(AXES, None, None),
        P(),
        P(AXES, None, None),
        P(),
    )
    return jax.shard_map(
        body,
        mesh=mesh,
        in_specs=placed,
        out_specs=(P(AXES, None, None), P()),
        check_vma=False,
    )
```

profile of v0, /device:TPU:15, one launch (start us, length us, event | category | flops | bytes accessed | tf_op | source)
XLA Modules:
  0.0 657.9 jit_solution(5763246498834404297)
XLA Ops:
  1.4 3.1 negate_multiply_fusion
  6.0 2.1 fusion.5.a_ref
  8.1 24.0 %spd_inverse.8 = f32[384,384]{1,0:T(8,128)} custom-call(f32[384,384]{1,0:T(8,128)} %fusion.5.a_ref), custom_call_target="tpu_custom_call" | custom-call | flops 16986931200 | bytes 1179648 | tf_op jit(solution)/shard_map/spd_inverse/pallas_call | solution.py:117
  35.8 7.9 %collective-permute-start.36 = (f32[384,128]{1,0:T(8,128)}, f32[384,128]{1,0:T(8,128)}, u32[]{:S(2)}, u32[]{:S(2)}) collective-permute-start(f32[384,128]{1,0:T(8,128)} %convolution_subtract_fusion.23), channel_id=1, source_target_pairs={{1,0},{2,1},{3,2},{4,3},{5,4},{6,5},{7,6},{8,7},{9,8},{10,9},{11,1... | collective-permute-start | bytes 589832 | tf_op jit(solution)/shard_map/ppermute | solution.py:137
  47.6 2.2 fusion.1
  49.8 7.4 %collective-permute-start = (f32[384,384]{1,0:T(8,128)}, f32[384,384]{1,0:T(8,128)}, u32[]{:S(2)}, u32[]{:S(2)}) collective-permute-start(f32[384,384]{1,0:T(8,128)} %fusion.1), channel_id=1, source_target_pairs={{1,0},{2,1},{3,2},{4,3},{5,4},{6,5},{7,6},{8,7},{9,8},{10,9},{11,1... | collective-permute-start | bytes 1769480 | tf_op jit(solution)/shard_map/ppermute | solution.py:137
  59.8 2.2 collective-permute-start.3
  63.5 2.2 fusion.3
  65.6 7.4 %collective-permute-start.1 = (f32[384,384]{1,0:T(8,128)}, f32[384,384]{1,0:T(8,128)}, u32[]{:S(2)}, u32[]{:S(2)}) collective-permute-start(f32[384,384]{1,0:T(8,128)} %fusion.3), channel_id=1, source_target_pairs={{1,0},{2,1},{3,2},{4,3},{5,4},{6,5},{7,6},{8,7},{9,8},{10,9},{11,1... | collective-permute-start | bytes 1769480 | tf_op jit(solution)/shard_map/ppermute | solution.py:137
  73.1 2.4 convolution_bitcast_fusion.2
  75.4 2.1 convolution_subtract_fusion.9
  79.6 2.9 convolution_negate_fusion.1
  84.3 11.1 %collective-permute-done.1 = f32[384,384]{1,0:T(8,128)} collective-permute-done((f32[384,384]{1,0:T(8,128)}, f32[384,384]{1,0:T(8,128)}, u32[]{:S(2)}, u32[]{:S(2)}) %collective-permute-start.1) | collective-permute-done | bytes 589856 | tf_op jit(solution)/shard_map/ppermute | solution.py:137
  95.4 3.1 fusion.2.a_ref
  98.5 24.2 %spd_inverse.9 = f32[384,384]{1,0:T(8,128)} custom-call(f32[384,384]{1,0:T(8,128)} %fusion.2.a_ref), custom_call_target="tpu_custom_call" | custom-call | flops 16986931200 | bytes 1179648 | tf_op jit(solution)/shard_map/spd_inverse/pallas_call | solution.py:117
  124.4 2.6 fusion
  135.5 8.1 %collective-permute-start.38 = (f32[384,128]{1,0:T(8,128)}, f32[384,128]{1,0:T(8,128)}, u32[]{:S(2)}, u32[]{:S(2)}) collective-permute-start(f32[384,128]{1,0:T(8,128)} %fusion.89), channel_id=1, source_target_pairs={{0,1},{2,3},{4,5},{6,7},{8,9},{10,11},{12,13},{14,15},{16,17},{18,... | collective-permute-start | bytes 589832 | tf_op jit(solution)/shard_map/ppermute | solution.py:137
  143.6 6.7 %collective-permute-start.39 = (f32[384,128]{1,0:T(8,128)}, f32[384,128]{1,0:T(8,128)}, u32[]{:S(2)}, u32[]{:S(2)}) collective-permute-start(f32[384,128]{1,0:T(8,128)} %fusion.90), channel_id=1, source_target_pairs={{2,1},{4,3},{6,5},{8,7},{10,9},{12,11},{14,13},{16,15},{18,17},{20... | collective-permute-start | bytes 589832 | tf_op jit(solution)/shard_map/ppermute | solution.py:137
  151.6 2.1 fusion.50
  153.7 6.8 %collective-permute-start.7 = (f32[384,384]{1,0:T(8,128)S(1)}, f32[384,384]{1,0:T(8,128)S(1)}, u32[]{:S(2)}, u32[]{:S(2)}) collective-permute-start(f32[384,384]{1,0:T(8,128)S(1)} %fusion.54), channel_id=1, source_target_pairs={{2,1},{4,3},{6,5},{8,7},{10,9},{12,11},{14,13},{16,15},{18,17},{20... | collective-permute-start | bytes 1769480 | tf_op jit(solution)/shard_map/ppermute | solution.py:137
  165.8 2.1 fusion.56
  168.0 2.2 convolution_subtract_fusion.4
  170.1 2.1 fusion.49
  172.3 7.6 %collective-permute-start.5 = (f32[384,384]{1,0:T(8,128)}, f32[384,384]{1,0:T(8,128)S(1)}, u32[]{:S(2)}, u32[]{:S(2)}) collective-permute-start(f32[384,384]{1,0:T(8,128)} %fusion.50), channel_id=1, source_target_pairs={{2,1},{4,3},{6,5},{8,7},{10,9},{12,11},{14,13},{16,15},{18,17},{20... | collective-permute-start | bytes 1769480 | tf_op jit(solution)/shard_map/ppermute | solution.py:137
  181.9 5.5 collective-permute-done.6
  189.6 24.0 %spd_inverse.10 = f32[384,384]{1,0:T(8,128)} custom-call(f32[384,384]{1,0:T(8,128)} %subtract_subtract_fusion.8.a_ref), custom_call_target="tpu_custom_call" | custom-call | flops 16986931200 | bytes 1179648 | tf_op jit(solution)/shard_map/spd_inverse/pallas_call | solution.py:117
  213.6 11.7 %collective-permute-done.9 = f32[384,384]{1,0:T(8,128)S(1)} collective-permute-done((f32[384,384]{1,0:T(8,128)}, f32[384,384]{1,0:T(8,128)S(1)}, u32[]{:S(2)}, u32[]{:S(2)}) %collective-permute-start.9) | collective-permute-done | bytes 589856 | tf_op jit(solution)/shard_map/ppermute | solution.py:137
  233.7 4.9 collective-permute-start.40
  238.7 2.4 collective-permute-start.42
  245.1 11.1 %collective-permute-start.8 = (f32[384,384]{1,0:T(8,128)S(1)}, f32[384,384]{1,0:T(8,128)S(1)}, u32[]{:S(2)}, u32[]{:S(2)}) collective-permute-start(f32[384,384]{1,0:T(8,128)S(1)} %convolution_subtract_fusion.3), channel_id=1, source_target_pairs={{1,3},{5,7},{9,11},{13,15},{17,19},{21,23},{25,27},{29,31}} | collective-permute-start | bytes 1769480 | tf_op jit(solution)/shard_map/ppermute | solution.py:137
  257.5 2.5 collective-permute-start.14
  260.0 2.2 fusion.58
  263.5 5.2 collective-permute-start.41
  270.0 3.5 collective-permute-start.16
  278.1 2.1 fusion.57
  281.1 2.3 collective-permute-start.12
  284.3 5.8 collective-permute-start.11
  291.2 5.7 collective-permute-done.16
  298.1 11.5 %collective-permute-done.13 = f32[384,384]{1,0:T(8,128)S(1)} collective-permute-done((f32[384,384]{1,0:T(8,128)S(1)}, f32[384,384]{1,0:T(8,128)S(1)}, u32[]{:S(2)}, u32[]{:S(2)}) %collective-permute-start.13) | collective-permute-done | bytes 589856 | tf_op jit(solution)/shard_map/ppermute | solution.py:137
  310.5 24.0 %spd_inverse.11 = f32[384,384]{1,0:T(8,128)} custom-call(f32[384,384]{1,0:T(8,128)} %subtract_subtract_fusion.6.a_ref), custom_call_target="tpu_custom_call" | custom-call | flops 16986931200 | bytes 1179648 | tf_op jit(solution)/shard_map/spd_inverse/pallas_call | solution.py:117
  349.6 2.1 fusion.66
  368.4 24.0 %spd_inverse.12 = f32[384,384]{1,0:T(8,128)} custom-call(f32[384,384]{1,0:T(8,128)} %subtract_subtract_fusion.4.a_ref), custom_call_target="tpu_custom_call" | custom-call | flops 16986931200 | bytes 1179648 | tf_op jit(solution)/shard_map/spd_inverse/pallas_call | solution.py:117
  406.7 2.2 fusion.74
  427.5 24.1 %spd_inverse.13 = f32[384,384]{1,0:T(8,128)} custom-call(f32[384,384]{1,0:T(8,128)} %subtract_subtract_fusion.2.a_ref), custom_call_target="tpu_custom_call" | custom-call | flops 16986931200 | bytes 1179648 | tf_op jit(solution)/shard_map/spd_inverse/pallas_call | solution.py:117
  466.1 2.2 fusion.82
  468.3 2.3 fusion.83
  471.4 2.4 fusion.84
  474.6 2.2 convolution_subtract_fusion
  478.4 2.4 fusion.99
  480.8 3.1 fusion.81
  487.8 24.0 %spd_inverse.14 = f32[384,384]{1,0:T(8,128)} custom-call(f32[384,384]{1,0:T(8,128)} %subtract_subtract_fusion.a_ref), custom_call_target="tpu_custom_call" | custom-call | flops 16986931200 | bytes 1179648 | tf_op jit(solution)/shard_map/spd_inverse/pallas_call | solution.py:117
  516.5 3.2 select_add_fusion.a_ref
  519.7 24.0 %spd_inverse.15 = f32[384,384]{1,0:T(8,128)} custom-call(f32[384,384]{1,0:T(8,128)} %select_add_fusion.a_ref), custom_call_target="tpu_custom_call" | custom-call | flops 16986931200 | bytes 1179648 | tf_op jit(solution)/shard_map/spd_inverse/pallas_call | solution.py:117
  546.9 2.3 convolution_select_fusion
  550.5 2.2 fusion.12
  561.0 2.4 fusion.16
  580.3 31.8 %collective-permute-start.64 = (f32[384,128]{1,0:T(8,128)S(1)}, f32[384,128]{1,0:T(8,128)S(1)}, u32[]{:S(2)}, u32[]{:S(2)}) collective-permute-start(f32[384,128]{1,0:T(8,128)S(1)} %fusion.20), channel_id=1, source_target_pairs={{3,1},{7,5},{11,9},{15,13},{19,17},{23,21},{27,25},{31,29}} | collective-permute-start | bytes 589832 | tf_op jit(solution)/shard_map/ppermute | solution.py:137
  615.2 4.6 collective-permute-done.64
  620.5 3.8 collective-permute-done.63
  625.7 5.0 collective-permute-start.66
  630.6 7.0 %collective-permute-start.65 = (f32[384,128]{1,0:T(8,128)S(1)}, f32[384,128]{1,0:T(8,128)S(1)}, u32[]{:S(2)}, u32[]{:S(2)}) collective-permute-start(f32[384,128]{1,0:T(8,128)S(1)} %fusion.22), channel_id=1, source_target_pairs={{1,2},{3,4},{5,6},{7,8},{9,10},{11,12},{13,14},{15,16},{17,18},{19... | collective-permute-start | bytes 589832 | tf_op jit(solution)/shard_map/ppermute | solution.py:137
  639.1 2.7 collective-permute-done.65
  643.1 8.0 %collective-permute-start.67 = (f32[384,128]{1,0:T(8,128)S(1)}, f32[384,128]{1,0:T(8,128)S(1)}, u32[]{:S(2)}, u32[]{:S(2)}) collective-permute-start(f32[384,128]{1,0:T(8,128)S(1)} %fusion.24), channel_id=1, source_target_pairs={{0,1},{1,2},{2,3},{3,4},{4,5},{5,6},{6,7},{7,8},{8,9},{9,10},{10,1... | collective-permute-start | bytes 589832 | tf_op jit(solution)/shard_map/ppermute | solution.py:137
  651.8 4.5 collective-permute-done.67
  (392 shorter events, 193.3 us)
Async XLA Ops:
  35.8 46.7 %collective-permute-start.36 = (f32[384,128]{1,0:T(8,128)}, f32[384,128]{1,0:T(8,128)}, u32[]{:S(2)}, u32[]{:S(2)}) collective-permute-start(f32[384,128]{1,0:T(8,128)} %convolution_subtract_fusion.23), channel_id=1, source_target_pairs={{1,0},{2,1},{3,2},{4,3},{5,4},{6,5},{7,6},{8,7},{9,8},{10,9},{11,1... | collective-permute-start | bytes 589832 | tf_op jit(solution)/shard_map/ppermute | solution.py:137
  49.8 74.6 %collective-permute-start = (f32[384,384]{1,0:T(8,128)}, f32[384,384]{1,0:T(8,128)}, u32[]{:S(2)}, u32[]{:S(2)}) collective-permute-start(f32[384,384]{1,0:T(8,128)} %fusion.1), channel_id=1, source_target_pairs={{1,0},{2,1},{3,2},{4,3},{5,4},{6,5},{7,6},{8,7},{9,8},{10,9},{11,1... | collective-permute-start | bytes 1769480 | tf_op jit(solution)/shard_map/ppermute | solution.py:137
  59.8 74.3 %collective-permute-start.3 = (f32[384,384]{1,0:T(8,128)S(1)}, f32[384,384]{1,0:T(8,128)S(1)}, u32[]{:S(2)}, u32[]{:S(2)}) collective-permute-start(f32[384,384]{1,0:T(8,128)S(1)} %convolution_negate_fusion), channel_id=1, source_target_pairs={{1,0},{3,2},{5,4},{7,6},{9,8},{11,10},{13,12},{15,14},{17,16},{19,... | collective-permute-start | bytes 1769480 | tf_op jit(solution)/shard_map/ppermute | solution.py:137
  65.6 29.7 %collective-permute-start.1 = (f32[384,384]{1,0:T(8,128)}, f32[384,384]{1,0:T(8,128)}, u32[]{:S(2)}, u32[]{:S(2)}) collective-permute-start(f32[384,384]{1,0:T(8,128)} %fusion.3), channel_id=1, source_target_pairs={{1,0},{2,1},{3,2},{4,3},{5,4},{6,5},{7,6},{8,7},{9,8},{10,9},{11,1... | collective-permute-start | bytes 1769480 | tf_op jit(solution)/shard_map/ppermute | solution.py:137
  130.0 42.3 %collective-permute-start.37 = (f32[384,128]{1,0:T(8,128)S(1)}, f32[384,128]{1,0:T(8,128)S(1)}, u32[]{:S(2)}, u32[]{:S(2)}) collective-permute-start(f32[384,128]{1,0:T(8,128)S(1)} %convolution_subtract_fusion.22), channel_id=1, source_target_pairs={{0,1},{2,3},{4,5},{6,7},{8,9},{10,11},{12,13},{14,15},{16,17},{18,... | collective-permute-start | bytes 589832 | tf_op jit(solution)/shard_map/ppermute | solution.py:137
  135.5 94.2 %collective-permute-start.38 = (f32[384,128]{1,0:T(8,128)}, f32[384,128]{1,0:T(8,128)}, u32[]{:S(2)}, u32[]{:S(2)}) collective-permute-start(f32[384,128]{1,0:T(8,128)} %fusion.89), channel_id=1, source_target_pairs={{0,1},{2,3},{4,5},{6,7},{8,9},{10,11},{12,13},{14,15},{16,17},{18,... | collective-permute-start | bytes 589832 | tf_op jit(solution)/shard_map/ppermute | solution.py:137
  143.6 86.1 %collective-permute-start.39 = (f32[384,128]{1,0:T(8,128)}, f32[384,128]{1,0:T(8,128)}, u32[]{:S(2)}, u32[]{:S(2)}) collective-permute-start(f32[384,128]{1,0:T(8,128)} %fusion.90), channel_id=1, source_target_pairs={{2,1},{4,3},{6,5},{8,7},{10,9},{12,11},{14,13},{16,15},{18,17},{20... | collective-permute-start | bytes 589832 | tf_op jit(solution)/shard_map/ppermute | solution.py:137
  153.7 26.8 %collective-permute-start.7 = (f32[384,384]{1,0:T(8,128)S(1)}, f32[384,384]{1,0:T(8,128)S(1)}, u32[]{:S(2)}, u32[]{:S(2)}) collective-permute-start(f32[384,384]{1,0:T(8,128)S(1)} %fusion.54), channel_id=1, source_target_pairs={{2,1},{4,3},{6,5},{8,7},{10,9},{12,11},{14,13},{16,15},{18,17},{20... | collective-permute-start | bytes 1769480 | tf_op jit(solution)/shard_map/ppermute | solution.py:137
  163.9 23.5 %collective-permute-start.6 = (f32[384,384]{1,0:T(8,128)S(1)}, f32[384,384]{1,0:T(8,128)S(1)}, u32[]{:S(2)}, u32[]{:S(2)}) collective-permute-start(f32[384,384]{1,0:T(8,128)S(1)} %fusion.52), channel_id=1, source_target_pairs={{0,1},{2,3},{4,5},{6,7},{8,9},{10,11},{12,13},{14,15},{16,17},{18,... | collective-permute-start | bytes 1769480 | tf_op jit(solution)/shard_map/ppermute | solution.py:137
  172.3 54.4 %collective-permute-start.5 = (f32[384,384]{1,0:T(8,128)}, f32[384,384]{1,0:T(8,128)S(1)}, u32[]{:S(2)}, u32[]{:S(2)}) collective-permute-start(f32[384,384]{1,0:T(8,128)} %fusion.50), channel_id=1, source_target_pairs={{2,1},{4,3},{6,5},{8,7},{10,9},{12,11},{14,13},{16,15},{18,17},{20... | collective-permute-start | bytes 1769480 | tf_op jit(solution)/shard_map/ppermute | solution.py:137
  180.6 47.8 %collective-permute-start.4 = (f32[384,384]{1,0:T(8,128)}, f32[384,384]{1,0:T(8,128)}, u32[]{:S(2)}, u32[]{:S(2)}) collective-permute-start(f32[384,384]{1,0:T(8,128)} %fusion.49), channel_id=1, source_target_pairs={{0,1},{2,3},{4,5},{6,7},{8,9},{10,11},{12,13},{14,15},{16,17},{18,... | collective-permute-start | bytes 1769480 | tf_op jit(solution)/shard_map/ppermute | solution.py:137
  187.4 37.9 %collective-permute-start.9 = (f32[384,384]{1,0:T(8,128)}, f32[384,384]{1,0:T(8,128)S(1)}, u32[]{:S(2)}, u32[]{:S(2)}) collective-permute-start(f32[384,384]{1,0:T(8,128)} %fusion.56), channel_id=1, source_target_pairs={{0,1},{2,3},{4,5},{6,7},{8,9},{10,11},{12,13},{14,15},{16,17},{18,... | collective-permute-start | bytes 1769480 | tf_op jit(solution)/shard_map/ppermute | solution.py:137
  225.3 18.3 %collective-permute-start.2 = (f32[384,384]{1,0:T(8,128)}, f32[384,384]{1,0:T(8,128)S(1)}, u32[]{:S(2)}, u32[]{:S(2)}) collective-permute-start(f32[384,384]{1,0:T(8,128)} %convolution_subtract_fusion.4), channel_id=1, source_target_pairs={{0,1},{2,3},{4,5},{6,7},{8,9},{10,11},{12,13},{14,15},{16,17},{18,... | collective-permute-start | bytes 1769480 | tf_op jit(solution)/shard_map/ppermute | solution.py:137
  226.7 36.2 %collective-permute-start.10 = (f32[384,384]{1,0:T(8,128)S(1)}, f32[384,384]{1,0:T(8,128)S(1)}, u32[]{:S(2)}, u32[]{:S(2)}) collective-permute-start(f32[384,384]{1,0:T(8,128)S(1)} %negate_select_fusion.3), channel_id=1, source_target_pairs={{3,1},{7,5},{11,9},{15,13},{19,17},{23,21},{27,25},{31,29}} | collective-permute-start | bytes 1769480 | tf_op jit(solution)/shard_map/ppermute | solution.py:137
  233.7 28.5 %collective-permute-start.40 = (f32[384,128]{1,0:T(8,128)S(1)}, f32[384,128]{1,0:T(8,128)S(1)}, u32[]{:S(2)}, u32[]{:S(2)}) collective-permute-start(f32[384,128]{1,0:T(8,128)S(1)} %convolution_subtract_fusion.21), channel_id=1, source_target_pairs={{1,3},{5,7},{9,11},{13,15},{17,19},{21,23},{25,27},{29,31}} | collective-permute-start | bytes 589832 | tf_op jit(solution)/shard_map/ppermute | solution.py:137
  238.7 42.5 %collective-permute-start.42 = (f32[384,128]{1,0:T(8,128)S(1)}, f32[384,128]{1,0:T(8,128)S(1)}, u32[]{:S(2)}, u32[]{:S(2)}) collective-permute-start(f32[384,128]{1,0:T(8,128)S(1)} %fusion.92), channel_id=1, source_target_pairs={{5,3},{9,7},{13,11},{17,15},{21,19},{25,23},{29,27}} | collective-permute-start | bytes 589832 | tf_op jit(solution)/shard_map/ppermute | solution.py:137
  245.1 31.7 %collective-permute-start.8 = (f32[384,384]{1,0:T(8,128)S(1)}, f32[384,384]{1,0:T(8,128)S(1)}, u32[]{:S(2)}, u32[]{:S(2)}) collective-permute-start(f32[384,384]{1,0:T(8,128)S(1)} %convolution_subtract_fusion.3), channel_id=1, source_target_pairs={{1,3},{5,7},{9,11},{13,15},{17,19},{21,23},{25,27},{29,31}} | collective-permute-start | bytes 1769480 | tf_op jit(solution)/shard_map/ppermute | solution.py:137
  257.5 40.7 %collective-permute-start.14 = (f32[384,384]{1,0:T(8,128)S(1)}, f32[384,384]{1,0:T(8,128)S(1)}, u32[]{:S(2)}, u32[]{:S(2)}) collective-permute-start(f32[384,384]{1,0:T(8,128)S(1)} %fusion.62), channel_id=1, source_target_pairs={{5,3},{9,7},{13,11},{17,15},{21,19},{25,23},{29,27}} | collective-permute-start | bytes 1769480 | tf_op jit(solution)/shard_map/ppermute | solution.py:137
  263.5 20.8 %collective-permute-start.41 = (f32[384,128]{1,0:T(8,128)S(1)}, f32[384,128]{1,0:T(8,128)S(1)}, u32[]{:S(2)}, u32[]{:S(2)}) collective-permute-start(f32[384,128]{1,0:T(8,128)S(1)} %fusion.91), channel_id=1, source_target_pairs={{1,3},{5,7},{9,11},{13,15},{17,19},{21,23},{25,27},{29,31}} | collective-permute-start | bytes 589832 | tf_op jit(solution)/shard_map/ppermute | solution.py:137
  270.0 27.0 %collective-permute-start.16 = (f32[384,384]{1,0:T(8,128)S(1)}, f32[384,384]{1,0:T(8,128)S(1)}, u32[]{:S(2)}, u32[]{:S(2)}) collective-permute-start(f32[384,384]{1,0:T(8,128)S(1)} %fusion.64), channel_id=1, source_target_pairs={{1,3},{5,7},{9,11},{13,15},{17,19},{21,23},{25,27},{29,31}} | collective-permute-start | bytes 1769480 | tf_op jit(solution)/shard_map/ppermute | solution.py:137
  276.8 32.8 %collective-permute-start.13 = (f32[384,384]{1,0:T(8,128)S(1)}, f32[384,384]{1,0:T(8,128)S(1)}, u32[]{:S(2)}, u32[]{:S(2)}) collective-permute-start(f32[384,384]{1,0:T(8,128)S(1)} %fusion.60), channel_id=1, source_target_pairs={{1,3},{5,7},{9,11},{13,15},{17,19},{21,23},{25,27},{29,31}} | collective-permute-start | bytes 1769480 | tf_op jit(solution)/shard_map/ppermute | solution.py:137
  281.1 58.2 %collective-permute-start.12 = (f32[384,384]{1,0:T(8,128)}, f32[384,384]{1,0:T(8,128)}, u32[]{:S(2)}, u32[]{:S(2)}) collective-permute-start(f32[384,384]{1,0:T(8,128)} %fusion.58), channel_id=1, source_target_pairs={{5,3},{9,7},{13,11},{17,15},{21,19},{25,23},{29,27}} | collective-permute-start | bytes 1769480 | tf_op jit(solution)/shard_map/ppermute | solution.py:137
  284.3 55.1 %collective-permute-start.11 = (f32[384,384]{1,0:T(8,128)}, f32[384,384]{1,0:T(8,128)}, u32[]{:S(2)}, u32[]{:S(2)}) collective-permute-start(f32[384,384]{1,0:T(8,128)} %fusion.57), channel_id=1, source_target_pairs={{1,3},{5,7},{9,11},{13,15},{17,19},{21,23},{25,27},{29,31}} | collective-permute-start | bytes 1769480 | tf_op jit(solution)/shard_map/ppermute | solution.py:137
  297.0 55.5 %collective-permute-start.17 = (f32[384,384]{1,0:T(8,128)S(1)}, f32[384,384]{1,0:T(8,128)S(1)}, u32[]{:S(2)}, u32[]{:S(2)}) collective-permute-start(f32[384,384]{1,0:T(8,128)S(1)} %negate_select_fusion.2), channel_id=1, source_target_pairs={{7,3},{15,11},{23,19},{31,27}} | collective-permute-start | bytes 1769480 | tf_op jit(solution)/shard_map/ppermute | solution.py:137
  343.4 8.4 %collective-permute-start.43 = (f32[384,128]{1,0:T(8,128)S(1)}, f32[384,128]{1,0:T(8,128)S(1)}, u32[]{:S(2)}, u32[]{:S(2)}) collective-permute-start(f32[384,128]{1,0:T(8,128)S(1)} %convolution_subtract_fusion.20), channel_id=1, source_target_pairs={{3,7},{11,15},{19,23},{27,31}} | collective-permute-start | bytes 589832 | tf_op jit(solution)/shard_map/ppermute | solution.py:137
  344.0 48.4 %collective-permute-start.45 = (f32[384,128]{1,0:T(8,128)}, f32[384,128]{1,0:T(8,128)}, u32[]{:S(2)}, u32[]{:S(2)}) collective-permute-start(f32[384,128]{1,0:T(8,128)} %fusion.95), channel_id=1, source_target_pairs={{11,7},{19,15},{27,23}} | collective-permute-start | bytes 589832 | tf_op jit(solution)/shard_map/ppermute | solution.py:137
  346.7 12.3 %collective-permute-start.15 = (f32[384,384]{1,0:T(8,128)S(1)}, f32[384,384]{1,0:T(8,128)S(1)}, u32[]{:S(2)}, u32[]{:S(2)}) collective-permute-start(f32[384,384]{1,0:T(8,128)S(1)} %convolution_subtract_fusion.2), channel_id=1, source_target_pairs={{3,7},{11,15},{19,23},{27,31}} | collective-permute-start | bytes 1769480 | tf_op jit(solution)/shard_map/ppermute | solution.py:137
  348.9 16.2 %collective-permute-start.21 = (f32[384,384]{1,0:T(8,128)S(1)}, f32[384,384]{1,0:T(8,128)S(1)}, u32[]{:S(2)}, u32[]{:S(2)}) collective-permute-start(f32[384,384]{1,0:T(8,128)S(1)} %fusion.70), channel_id=1, source_target_pairs={{11,7},{19,15},{27,23}} | collective-permute-start | bytes 1769480 | tf_op jit(solution)/shard_map/ppermute | solution.py:137
  353.7 9.8 %collective-permute-start.23 = (f32[384,384]{1,0:T(8,128)S(1)}, f32[384,384]{1,0:T(8,128)S(1)}, u32[]{:S(2)}, u32[]{:S(2)}) collective-permute-start(f32[384,384]{1,0:T(8,128)S(1)} %fusion.72), channel_id=1, source_target_pairs={{3,7},{11,15},{19,23},{27,31}} | collective-permute-start | bytes 1769480 | tf_op jit(solution)/shard_map/ppermute | solution.py:137
  357.0 9.6 %collective-permute-start.20 = (f32[384,384]{1,0:T(8,128)S(1)}, f32[384,384]{1,0:T(8,128)S(1)}, u32[]{:S(2)}, u32[]{:S(2)}) collective-permute-start(f32[384,384]{1,0:T(8,128)S(1)} %fusion.68), channel_id=1, source_target_pairs={{3,7},{11,15},{19,23},{27,31}} | collective-permute-start | bytes 1769480 | tf_op jit(solution)/shard_map/ppermute | solution.py:137
  359.0 37.8 %collective-permute-start.19 = (f32[384,384]{1,0:T(8,128)}, f32[384,384]{1,0:T(8,128)}, u32[]{:S(2)}, u32[]{:S(2)}) collective-permute-start(f32[384,384]{1,0:T(8,128)} %fusion.66), channel_id=1, source_target_pairs={{11,7},{19,15},{27,23}} | collective-permute-start | bytes 1769480 | tf_op jit(solution)/shard_map/ppermute | solution.py:137
  363.5 28.9 %collective-permute-start.44 = (f32[384,128]{1,0:T(8,128)}, f32[384,128]{1,0:T(8,128)}, u32[]{:S(2)}, u32[]{:S(2)}) collective-permute-start(f32[384,128]{1,0:T(8,128)} %fusion.94), channel_id=1, source_target_pairs={{3,7},{11,15},{19,23},{27,31}} | collective-permute-start | bytes 589832 | tf_op jit(solution)/shard_map/ppermute | solution.py:137
  365.1 31.8 %collective-permute-start.18 = (f32[384,384]{1,0:T(8,128)}, f32[384,384]{1,0:T(8,128)}, u32[]{:S(2)}, u32[]{:S(2)}) collective-permute-start(f32[384,384]{1,0:T(8,128)} %fusion.65), channel_id=1, source_target_pairs={{3,7},{11,15},{19,23},{27,31}} | collective-permute-start | bytes 1769480 | tf_op jit(solution)/shard_map/ppermute | solution.py:137
  366.6 43.0 %collective-permute-start.24 = (f32[384,384]{1,0:T(8,128)S(1)}, f32[384,384]{1,0:T(8,128)S(1)}, u32[]{:S(2)}, u32[]{:S(2)}) collective-permute-start(f32[384,384]{1,0:T(8,128)S(1)} %negate_select_fusion.1), channel_id=1, source_target_pairs={{15,7},{31,23}} | collective-permute-start | bytes 1769480 | tf_op jit(solution)/shard_map/ppermute | solution.py:137
  400.9 8.0 %collective-permute-start.46 = (f32[384,128]{1,0:T(8,128)S(1)}, f32[384,128]{1,0:T(8,128)S(1)}, u32[]{:S(2)}, u32[]{:S(2)}) collective-permute-start(f32[384,128]{1,0:T(8,128)S(1)} %convolution_subtract_fusion.19), channel_id=1, source_target_pairs={{7,15},{23,31}} | collective-permute-start | bytes 589832 | tf_op jit(solution)/shard_map/ppermute | solution.py:137
  401.5 18.4 %collective-permute-start.48 = (f32[384,128]{1,0:T(8,128)S(1)}, f32[384,128]{1,0:T(8,128)S(1)}, u32[]{:S(2)}, u32[]{:S(2)}) collective-permute-start(f32[384,128]{1,0:T(8,128)S(1)} %fusion.97), channel_id=1, source_target_pairs={{23,15}} | collective-permute-start | bytes 589832 | tf_op jit(solution)/shard_map/ppermute | solution.py:137
  403.6 12.7 %collective-permute-start.22 = (f32[384,384]{1,0:T(8,128)S(1)}, f32[384,384]{1,0:T(8,128)S(1)}, u32[]{:S(2)}, u32[]{:S(2)}) collective-permute-start(f32[384,384]{1,0:T(8,128)S(1)} %convolution_subtract_fusion.1), channel_id=1, source_target_pairs={{7,15},{23,31}} | collective-permute-start | bytes 1769480 | tf_op jit(solution)/shard_map/ppermute | solution.py:137
  406.0 20.6 %collective-permute-start.28 = (f32[384,384]{1,0:T(8,128)S(1)}, f32[384,384]{1,0:T(8,128)S(1)}, u32[]{:S(2)}, u32[]{:S(2)}) collective-permute-start(f32[384,384]{1,0:T(8,128)S(1)} %fusion.78), channel_id=1, source_target_pairs={{23,15}} | collective-permute-start | bytes 1769480 | tf_op jit(solution)/shard_map/ppermute | solution.py:137
  410.2 11.3 %collective-permute-start.47 = (f32[384,128]{1,0:T(8,128)S(1)}, f32[384,128]{1,0:T(8,128)S(1)}, u32[]{:S(2)}, u32[]{:S(2)}) collective-permute-start(f32[384,128]{1,0:T(8,128)S(1)} %fusion.96), channel_id=1, source_target_pairs={{7,15},{23,31}} | collective-permute-start | bytes 589832 | tf_op jit(solution)/shard_map/ppermute | solution.py:137
  412.1 12.6 %collective-permute-start.30 = (f32[384,384]{1,0:T(8,128)S(1)}, f32[384,384]{1,0:T(8,128)S(1)}, u32[]{:S(2)}, u32[]{:S(2)}) collective-permute-start(f32[384,384]{1,0:T(8,128)S(1)} %fusion.80), channel_id=1, source_target_pairs={{7,15},{23,31}} | collective-permute-start | bytes 1769480 | tf_op jit(solution)/shard_map/ppermute | solution.py:137
  416.3 10.3 %collective-permute-start.27 = (f32[384,384]{1,0:T(8,128)S(1)}, f32[384,384]{1,0:T(8,128)S(1)}, u32[]{:S(2)}, u32[]{:S(2)}) collective-permute-start(f32[384,384]{1,0:T(8,128)S(1)} %fusion.76), channel_id=1, source_target_pairs={{7,15},{23,31}} | collective-permute-start | bytes 1769480 | tf_op jit(solution)/shard_map/ppermute | solution.py:137
  420.0 36.5 %collective-permute-start.26 = (f32[384,384]{1,0:T(8,128)}, f32[384,384]{1,0:T(8,128)}, u32[]{:S(2)}, u32[]{:S(2)}) collective-permute-start(f32[384,384]{1,0:T(8,128)} %fusion.74), channel_id=1, source_target_pairs={{23,15}} | collective-permute-start | bytes 1769480 | tf_op jit(solution)/shard_map/ppermute | solution.py:137
  421.5 35.0 %collective-permute-start.25 = (f32[384,384]{1,0:T(8,128)}, f32[384,384]{1,0:T(8,128)}, u32[]{:S(2)}, u32[]{:S(2)}) collective-permute-start(f32[384,384]{1,0:T(8,128)} %fusion.73), channel_id=1, source_target_pairs={{7,15},{23,31}} | collective-permute-start | bytes 1769480 | tf_op jit(solution)/shard_map/ppermute | solution.py:137
  424.8 43.5 %collective-permute-start.31 = (f32[384,384]{1,0:T(8,128)S(1)}, f32[384,384]{1,0:T(8,128)}, u32[]{:S(2)}, u32[]{:S(2)}) collective-permute-start(f32[384,384]{1,0:T(8,128)S(1)} %negate_select_fusion), channel_id=1, source_target_pairs={{31,15}} | collective-permute-start | bytes 1769480 | tf_op jit(solution)/shard_map/ppermute | solution.py:137
  459.9 86.9 %collective-permute-start.49 = (f32[384,128]{1,0:T(8,128)}, f32[384,128]{1,0:T(8,128)}, u32[]{:S(2)}, u32[]{:S(2)}) collective-permute-start(f32[384,128]{1,0:T(8,128)} %convolution_subtract_fusion.18), channel_id=1, source_target_pairs={{15,31}} | collective-permute-start | bytes 589832 | tf_op jit(solution)/shard_map/ppermute | solution.py:137
  461.3 82.4 %collective-permute-start.51 = (f32[384,128]{1,0:T(8,128)}, f32[384,128]{1,0:T(8,128)}, u32[]{:S(2)}, u32[]{:S(2)}) collective-permute-start(f32[384,128]{1,0:T(8,128)} %fusion.100), channel_id=1, source_target_pairs={} | collective-permute-start | bytes 589832 | tf_op jit(solution)/shard_map/ppermute | solution.py:137
  463.9 20.0 %collective-permute-start.35 = (f32[384,384]{1,0:T(8,128)S(1)}, f32[384,384]{1,0:T(8,128)S(1)}, u32[]{:S(2)}, u32[]{:S(2)}) collective-permute-start(f32[384,384]{1,0:T(8,128)S(1)} %fusion.86), channel_id=1, source_target_pairs={} | collective-permute-start | bytes 1769480 | tf_op jit(solution)/shard_map/ppermute | solution.py:137
  473.8 11.5 %collective-permute-start.34 = (f32[384,384]{1,0:T(8,128)S(1)}, f32[384,384]{1,0:T(8,128)S(1)}, u32[]{:S(2)}, u32[]{:S(2)}) collective-permute-start(f32[384,384]{1,0:T(8,128)S(1)} %fusion.84), channel_id=1, source_target_pairs={{15,31}} | collective-permute-start | bytes 1769480 | tf_op jit(solution)/shard_map/ppermute | solution.py:137
  476.7 39.7 %collective-permute-start.29 = (f32[384,384]{1,0:T(8,128)}, f32[384,384]{1,0:T(8,128)}, u32[]{:S(2)}, u32[]{:S(2)}) collective-permute-start(f32[384,384]{1,0:T(8,128)} %convolution_subtract_fusion), channel_id=1, source_target_pairs={{15,31}} | collective-permute-start | bytes 1769480 | tf_op jit(solution)/shard_map/ppermute | solution.py:137
  483.9 27.9 %collective-permute-start.33 = (f32[384,384]{1,0:T(8,128)}, f32[384,384]{1,0:T(8,128)}, u32[]{:S(2)}, u32[]{:S(2)}) collective-permute-start(f32[384,384]{1,0:T(8,128)} %fusion.82), channel_id=1, source_target_pairs={} | collective-permute-start | bytes 1769480 | tf_op jit(solution)/shard_map/ppermute | solution.py:137
  485.4 28.4 %collective-permute-start.32 = (f32[384,384]{1,0:T(8,128)}, f32[384,384]{1,0:T(8,128)}, u32[]{:S(2)}, u32[]{:S(2)}) collective-permute-start(f32[384,384]{1,0:T(8,128)} %fusion.81), channel_id=1, source_target_pairs={{15,31}} | collective-permute-start | bytes 1769480 | tf_op jit(solution)/shard_map/ppermute | solution.py:137
  511.9 31.8 %collective-permute-start.50 = (f32[384,128]{1,0:T(8,128)}, f32[384,128]{1,0:T(8,128)}, u32[]{:S(2)}, u32[]{:S(2)}) collective-permute-start(f32[384,128]{1,0:T(8,128)} %fusion.99), channel_id=1, source_target_pairs={{15,31}} | collective-permute-start | bytes 589832 | tf_op jit(solution)/shard_map/ppermute | solution.py:137
  553.5 5.8 collective-permute-start.57
  556.0 9.7 %collective-permute-start.53 = (f32[384,128]{1,0:T(8,128)}, f32[384,128]{1,0:T(8,128)}, u32[]{:S(2)}, u32[]{:S(2)}) collective-permute-start(f32[384,128]{1,0:T(8,128)} %add.161), channel_id=1, source_target_pairs={{15,7},{31,23}} | collective-permute-start | bytes 589832 | tf_op jit(solution)/shard_map/ppermute | solution.py:137
  563.4 5.4 collective-permute-start.60
  564.9 5.5 collective-permute-start.59
  567.4 7.6 %collective-permute-start.54 = (f32[384,128]{1,0:T(8,128)}, f32[384,128]{1,0:T(8,128)}, u32[]{:S(2)}, u32[]{:S(2)}) collective-permute-start(f32[384,128]{1,0:T(8,128)} %add.162), channel_id=1, source_target_pairs={{7,3},{15,11},{23,19},{31,27}} | collective-permute-start | bytes 589832 | tf_op jit(solution)/shard_map/ppermute | solution.py:137
  576.1 37.4 %collective-permute-start.55 = (f32[384,128]{1,0:T(8,128)S(1)}, f32[384,128]{1,0:T(8,128)S(1)}, u32[]{:S(2)}, u32[]{:S(2)}) collective-permute-start(f32[384,128]{1,0:T(8,128)S(1)} %add.163), channel_id=1, source_target_pairs={{3,1},{7,5},{11,9},{15,13},{19,17},{23,21},{27,25},{31,29}} | collective-permute-start | bytes 589832 | tf_op jit(solution)/shard_map/ppermute | solution.py:137
  580.3 39.5 %collective-permute-start.64 = (f32[384,128]{1,0:T(8,128)S(1)}, f32[384,128]{1,0:T(8,128)S(1)}, u32[]{:S(2)}, u32[]{:S(2)}) collective-permute-start(f32[384,128]{1,0:T(8,128)S(1)} %fusion.20), channel_id=1, source_target_pairs={{3,1},{7,5},{11,9},{15,13},{19,17},{23,21},{27,25},{31,29}} | collective-permute-start | bytes 589832 | tf_op jit(solution)/shard_map/ppermute | solution.py:137
  612.1 12.2 %collective-permute-start.63 = (f32[384,128]{1,0:T(8,128)S(1)}, f32[384,128]{1,0:T(8,128)S(1)}, u32[]{:S(2)}, u32[]{:S(2)}) collective-permute-start(f32[384,128]{1,0:T(8,128)S(1)} %fusion.20), channel_id=1, source_target_pairs={{3,5},{7,9},{11,13},{15,17},{19,21},{23,25},{27,29}} | collective-permute-start | bytes 589832 | tf_op jit(solution)/shard_map/ppermute | solution.py:137
  613.6 24.1 %collective-permute-start.56 = (f32[384,128]{1,0:T(8,128)S(1)}, f32[384,128]{1,0:T(8,128)S(1)}, u32[]{:S(2)}, u32[]{:S(2)}) collective-permute-start(f32[384,128]{1,0:T(8,128)S(1)} %add.164), channel_id=1, source_target_pairs={{1,0},{3,2},{5,4},{7,6},{9,8},{11,10},{13,12},{15,14},{17,16},{19,... | collective-permute-start | bytes 589832 | tf_op jit(solution)/shard_map/ppermute | solution.py:137
  625.7 12.8 %collective-permute-start.66 = (f32[384,128]{1,0:T(8,128)S(1)}, f32[384,128]{1,0:T(8,128)S(1)}, u32[]{:S(2)}, u32[]{:S(2)}) collective-permute-start(f32[384,128]{1,0:T(8,128)S(1)} %fusion.22), channel_id=1, source_target_pairs={{1,0},{3,2},{5,4},{7,6},{9,8},{11,10},{13,12},{15,14},{17,16},{19,... | collective-permute-start | bytes 589832 | tf_op jit(solution)/shard_map/ppermute | solution.py:137
  630.6 11.1 %collective-permute-start.65 = (f32[384,128]{1,0:T(8,128)S(1)}, f32[384,128]{1,0:T(8,128)S(1)}, u32[]{:S(2)}, u32[]{:S(2)}) collective-permute-start(f32[384,128]{1,0:T(8,128)S(1)} %fusion.22), channel_id=1, source_target_pairs={{1,2},{3,4},{5,6},{7,8},{9,10},{11,12},{13,14},{15,16},{17,18},{19... | collective-permute-start | bytes 589832 | tf_op jit(solution)/shard_map/ppermute | solution.py:137
  643.1 13.2 %collective-permute-start.67 = (f32[384,128]{1,0:T(8,128)S(1)}, f32[384,128]{1,0:T(8,128)S(1)}, u32[]{:S(2)}, u32[]{:S(2)}) collective-permute-start(f32[384,128]{1,0:T(8,128)S(1)} %fusion.24), channel_id=1, source_target_pairs={{0,1},{1,2},{2,3},{3,4},{4,5},{5,6},{6,7},{7,8},{8,9},{9,10},{10,1... | collective-permute-start | bytes 589832 | tf_op jit(solution)/shard_map/ppermute | solution.py:137
  (90 other events, 912.1 us)
where the time goes:
time: 671 us; the launch traced here: 658 us
  starting transfers between devices  200 us (30%)
  Pallas kernels  192 us (29%)
  matrix products  165 us (25%)
  waiting for transfers between devices  62.1 us (9%)
  other arithmetic  29.8 us (4%)
    ppermute x68, starting transfers between devices, send(): return lax.ppermute(values, AXES, pairs)  200 us
    pallas_call x8, Pallas kernels, spd_inverse(): pl.pallas_call(inverse_kernel, out_shape=jax.ShapeDtypeStruct(matrix.shap...  192 us
    dot_general x56, matrix products, gram_prod(): return jnp.einsum('ji,jk->ik', left, right, precision=precision)  94.9 us
    dot_general x49, matrix products, mat_prod(): return jnp.matmul(left, right, precision=precision)  68.2 us
    ppermute x68, waiting for transfers between devices, send(): return lax.ppermute(values, AXES, pairs)  62.1 us
  transfers between devices with their start and end apart: 68, of which 10 were waited for; matrix products, arithmetic and copies ran while one was open for 27% of the time, Pallas kernels for 26%

commit v1 on v0

v1 whole, which is shorter than its diff:
```python
import functools

import jax
import jax.numpy as jnp
from jax import lax
from jax.experimental import pallas as pl
from jax.experimental.pallas import tpu as pltpu
from jax.sharding import PartitionSpec as P

AXES = ("long", "short")
PREC = lax.Precision.HIGHEST
LANES = 128
SUBLANES = 8
MESH = pl.DeviceIdType.MESH
F32 = jnp.float32


def dot(left, right):
    return jnp.dot(left, right, precision=PREC, preferred_element_type=F32)


def gram(left, right):
    return lax.dot_general(
        left, right, (((0,), (0,)), ((), ())), precision=PREC, preferred_element_type=F32
    )


def inverse_two(a, b, c):
    inv = 1.0 / (a * c - b * b)
    return c * inv, -(b * inv), a * inv


def pivot_four(tiles, first, lane, sub):
    group, row = divmod(first, SUBLANES)
    shape = (SUBLANES, LANES)
    cols = [
        [jnp.broadcast_to(t[:, first + k : first + k + 1], shape) for t in tiles] for k in range(4)
    ]

    def entry(i, k):
        return cols[k][group][row + i : row + i + 1, :]

    a00, a01, a11 = inverse_two(entry(0, 0), entry(0, 1), entry(1, 1))
    b00, b01, b10, b11 = entry(0, 2), entry(0, 3), entry(1, 2), entry(1, 3)
    m00, m01 = a00 * b00 + a01 * b10, a00 * b01 + a01 * b11
    m10, m11 = a01 * b00 + a11 * b10, a01 * b01 + a11 * b11
    s00, s01, s11 = inverse_two(
        entry(2, 2) - (b00 * m00 + b10 * m10),
        entry(2, 3) - (b00 * m01 + b10 * m11),
        entry(3, 3) - (b01 * m01 + b11 * m11),
    )
    u00, u01 = m00 * s00 + m01 * s01, m00 * s01 + m01 * s11
    u10, u11 = m10 * s00 + m11 * s01, m10 * s01 + m11 * s11
    t01 = a01 + (u00 * m10 + u01 * m11)
    pivot_inverse = (
        (a00 + (u00 * m00 + u01 * m01), t01, -u00, -u01),
        (t01, a11 + (u10 * m10 + u11 * m11), -u10, -u11),
        (-u00, -u10, s00, s01),
        (-u01, -u11, s01, s11),
    )
    inside = jnp.logical_and(lane >= first, lane < first + 4)
    rows = [
        jnp.where(
            inside[:1],
            jnp.where(lane[:1] == first + k, 1.0, 0.0),
            tiles[group][row + k : row + k + 1, :],
        )
        for k in range(4)
    ]
    scaled = [
        jnp.broadcast_to(
            (p[0] * rows[0] + p[1] * rows[1]) + (p[2] * rows[2] + p[3] * rows[3]), shape
        )
        for p in pivot_inverse
    ]
    out = []
    for place, tile in enumerate(tiles):
        new = jnp.where(inside, 0.0, tile)
        for k in range(4):
            new = new - cols[k][place] * scaled[k]
        if place == group:
            for k in range(4):
                new = jnp.where(sub == row + k, scaled[k], new)
        out.append(new)
    return out


def invert(o_ref):
    width = o_ref.shape[0]
    lane = lax.broadcasted_iota(jnp.int32, (SUBLANES, LANES), 1)
    sub = lax.broadcasted_iota(jnp.int32, (SUBLANES, LANES), 0)

    def step(k, carry):
        at = pl.multiple_of(k * LANES, LANES)
        here = pl.ds(at, LANES)
        tiles = [
            o_ref[pl.ds(pl.multiple_of(at + SUBLANES * g, SUBLANES), SUBLANES), here]
            for g in range(LANES // SUBLANES)
        ]
        for first in range(0, LANES, 4):
            tiles = pivot_four(tiles, first, lane, sub)
        pivot = jnp.concatenate(tiles, axis=0)
        rows = o_ref[here, :]
        columns = o_ref[:, here]
        scaled = dot(pivot, rows)
        o_ref[here, :] = scaled
        o_ref[here, here] = pivot
        scaled = o_ref[here, :]
        o_ref[:, here] = jnp.zeros((width, LANES), F32)
        o_ref[...] = o_ref[...] - dot(columns, scaled)
        o_ref[here, :] = scaled
        return carry

    lax.fori_loop(0, width // LANES, step, 0)


def host_side(level, segment):
    if level == 0:
        return 1 - lax.rem(segment // 2, 2)
    if level == 1:
        return lax.rem(segment, 2)
    return 0


def host_of(level, segment):
    for low in reversed(range(level)):
        segment = 2 * segment + host_side(low, segment)
    return segment


def choose(values, index):
    picked = values[0]
    for k in range(1, len(values)):
        picked = jnp.where(index == k, values[k], picked)
    return picked


def column_of(row, width):
    turned = jnp.broadcast_to(row, (LANES, row.shape[1])).T
    return jnp.concatenate([turned] * (width // LANES), axis=1)


def diagonal(row):
    n = row.shape[1]
    at = lax.broadcasted_iota(jnp.int32, (n, n), 0)
    across = lax.broadcasted_iota(jnp.int32, (n, n), 1)
    return jnp.where(at == across, jnp.broadcast_to(row, (n, n)), 0.0)


def kernel(
    levels, shorts,
    trans, innov, observ, effects, prior, right, tip_right,
    out, tip_out,
    dd, ab, tip, work, abm, xs, ys, yab,
    near_d, near_ab, far_d, far_ab, got_tip, sol, tip_sol,
    send_sem, recv_sem, back_send, back_recv,
):
    n = trans.shape[1]
    k = effects.shape[2]
    m = right.shape[2]
    me = lax.axis_index("long") * shorts + lax.axis_index("short")

    segs = [me // (1 << v) for v in range(levels + 1)]
    halves = [lax.rem(s, 2) for s in segs]
    active = [host_of(v, segs[v]) == me for v in range(levels + 1)]
    partners = [host_of(v, segs[v] + 1 - 2 * halves[v]) for v in range(levels)]
    hosting = [active[v + 1] for v in range(levels)]
    sending = [jnp.logical_and(active[v], jnp.logical_not(active[v + 1])) for v in range(levels)]

    def place(position):
        return (position // shorts, lax.rem(position, shorts))

    barrier = pltpu.get_barrier_semaphore()
    for v in range(levels):
        @pl.when(active[v])
        def _():
            pl.semaphore_signal(barrier, inc=1, device_id=place(partners[v]), device_id_type=MESH)

    def forward_copy(what, v, side, far, target):
        parts = (
            (dd.at[side], near_d.at[v]),
            (xs.at[v + 1, far], xs.at[v + 1, far]),
            (ab.at[side], near_ab.at[v]),
            (dd.at[far], far_d.at[v]),
            (ab.at[far], far_ab.at[v]),
            (tip, got_tip.at[v]),
        )
        return pltpu.make_async_remote_copy(
            src_ref=parts[what][0],
            dst_ref=parts[what][1],
            send_sem=send_sem.at[what],
            recv_sem=recv_sem.at[v, what],
            device_id=place(target),
            device_id_type=MESH,
        )

    first = jnp.where(me == 0, 0.0, 1.0).astype(F32)
    trans_now = trans[0] * first
    weight_now = column_of(innov[0:1, :], n)
    weight_next = column_of(innov[1:2, :], n)
    scaled_next = weight_next * trans[1]
    work[...] = diagonal(innov[0:1, :] + observ[0:1, :]) + gram(trans[1], scaled_next)
    xs[0, 1] = -(scaled_next.T)
    scaled_now = weight_now * trans_now
    xs[0, 0] = -scaled_now
    dd[0] = gram(trans_now, scaled_now)
    dd[1] = diagonal(innov[1:2, :] + observ[1:2, :])

    count = active[0].astype(jnp.int32)
    for v in range(1, levels):
        count = count + active[v].astype(jnp.int32)
    pl.semaphore_wait(barrier, count)

    def stage(s, carry):
        last = levels
        below = jnp.maximum(s - 1, 0)
        half = choose(halves, below)
        near_now = 1 - half
        far_next = choose(halves, jnp.minimum(s, last))
        near_next = 1 - far_next
        runs = choose(active + [active[levels]] * 2, s)
        sends = jnp.logical_and(s < last, choose(sending + [sending[0]], jnp.minimum(s, last)))
        target = choose(partners, jnp.minimum(s, last - 1))
        merges = jnp.logical_and(s > 0, s <= last)

        def arrived(what):
            forward_copy(what, below, near_now, 1 - half, me).wait_recv()

        @pl.when(runs)
        def _():
            @pl.when(merges)
            def _():
                arrived(0)
                work[...] = dd[near_now] + near_d[below]

            @pl.when(s == last + 1)
            def _():
                work[...] = dd[1]

            @pl.when(s == last + 2)
            def _():
                work[...] = tip[:, :k] + diagonal(prior[...])

            invert(work)

            @pl.when(s <= last)
            def _():
                @pl.when(merges)
                def _():
                    arrived(1)
                    arrived(2)
                    abm[...] = ab[near_now] + near_ab[below]
                    arrived(3)
                    dd[near_now] = far_d[below]
                    arrived(4)
                    ab[near_now] = far_ab[below]

                ys[near_next] = dot(work[...], xs[s, near_next])
                dd[near_next] = dd[near_next] - gram(xs[s, near_next], ys[near_next])

                @pl.when(sends)
                def _():
                    forward_copy(0, s, near_next, far_next, target).start()

                ys[far_next] = dot(work[...], xs[s, far_next])

                @pl.when(s < last)
                def _():
                    xs[s + 1, far_next] = -gram(xs[s, near_next], ys[far_next])

                @pl.when(sends)
                def _():
                    forward_copy(1, s, near_next, far_next, target).start()

                @pl.when(s == 0)
                def _():
                    loaded_now = weight_col(0) * effects[0]
                    loaded_next = weight_col(1) * effects[1]
                    abm[:, :k] = gram(trans[1], loaded_next) - loaded_now
                    abm[:, k:] = right[0]
                    ab[0, :, :k] = gram(trans[0] * first, loaded_now)
                    ab[0, :, k:] = jnp.zeros((n, m), F32)
                    ab[1, :, :k] = -loaded_next
                    ab[1, :, k:] = right[1]
                    tip[:, :k] = gram(effects[0], loaded_now) + gram(effects[1], loaded_next)
                    tip[:, k:] = jnp.zeros((k, m), F32)

                yab[s] = dot(work[...], abm[...])
                ab[near_next] = ab[near_next] - gram(xs[s, near_next], yab[s])

                @pl.when(sends)
                def _():
                    forward_copy(2, s, near_next, far_next, target).start()

                dd[far_next] = dd[far_next] - gram(xs[s, far_next], ys[far_next])

                @pl.when(sends)
                def _():
                    forward_copy(3, s, near_next, far_next, target).start()

                ab[far_next] = ab[far_next] - gram(xs[s, far_next], yab[s])

                @pl.when(sends)
                def _():
                    forward_copy(4, s, near_next, far_next, target).start()

                tip[...] = tip[...] - gram(abm[:, :k], yab[s])
                xs[s, 0] = ys[0]
                xs[s, 1] = ys[1]

            @pl.when(s == last + 1)
            def _():
                yab[s] = dot(work[...], ab[1])
                tip[...] = tip[...] - gram(ab[1, :, :k], yab[s])

            @pl.when(jnp.logical_or(sends, s == last + 1))
            def _():
                for v in range(levels):
                    @pl.when(jnp.logical_and(hosting[v], v < s))
                    def _():
                        forward_copy(5, v, 0, 1, me).wait_recv()
                        tip[...] = tip[...] + got_tip[v]

            @pl.when(sends)
            def _():
                forward_copy(5, s, near_next, far_next, target).start()

            @pl.when(s == last + 2)
            def _():
                found = dot(work[...], tip[:, k:] + tip_right[...])
                tip_sol[...] = found
                sol[levels, 1] = yab[last + 1, :, k:] - dot(yab[last + 1, :, :k], found)
                sol[levels, 0] = jnp.zeros((n, m), F32)

        return carry

    def weight_col(t):
        return column_of(innov[t : t + 1, :], k)

    lax.fori_loop(0, levels + 3, stage, 0)

    def back_copy(what, v, half, target):
        other = 1 - half
        src = (tip_sol, sol.at[v + 1, other], sol.at[v, other])[what]
        dst = (tip_sol, sol.at[v, other], sol.at[v, half])[what]
        return pltpu.make_async_remote_copy(
            src_ref=src,
            dst_ref=dst,
            send_sem=back_send.at[v, what],
            recv_sem=back_recv.at[what],
            device_id=place(target),
            device_id_type=MESH,
        )

    def back(i, carry):
        v = levels - 1 - i
        half = choose(halves, v)
        hosts = choose(hosting, v)
        waits = choose(sending, v)
        target = choose(partners, v)

        @pl.when(hosts)
        def _():
            back_copy(0, v, half, target).start()
            back_copy(1, v, half, target).start()
            value = yab[v + 1, :, k:] - dot(yab[v + 1, :, :k], tip_sol[...])
            value = value - dot(xs[v + 1, 0], sol[v + 1, 0])
            sol[v, 1 - half] = value - dot(xs[v + 1, 1], sol[v + 1, 1])
            back_copy(2, v, half, target).start()
            sol[v, half] = sol[v + 1, half]

        @pl.when(waits)
        def _():
            for what in range(3):
                back_copy(what, v, 1 - half, me).wait_recv()

        return carry

    lax.fori_loop(0, levels, back, 0)

    value = yab[0, :, k:] - dot(yab[0, :, :k], tip_sol[...])
    value = value - dot(xs[0, 0], sol[0, 0])
    out[0] = value - dot(xs[0, 1], sol[0, 1])
    out[1] = sol[0, 1]
    tip_out[...] = tip_sol[...]

    for v in range(levels):
        @pl.when(sending[v])
        def _():
            for what in range(6):
                forward_copy(what, v, 1 - halves[v], halves[v], partners[v]).wait_send()

        @pl.when(hosting[v])
        def _():
            for what in range(3):
                back_copy(what, v, halves[v], partners[v]).wait_send()


def body(transition, innovation, observation, effects, prior, right_side, tip_right):
    blocks, n = innovation.shape
    k = prior.shape[0]
    m = right_side.shape[2]
    shorts = lax.axis_size("short")
    total = lax.axis_size(AXES)
    levels = total.bit_length() - 1
    assert blocks == 2 and total == 1 << levels
    vmem = pl.BlockSpec(memory_space=pltpu.VMEM)
    wide = k + m
    return pl.pallas_call(
        functools.partial(kernel, levels, shorts),
        out_shape=(
            jax.ShapeDtypeStruct(right_side.shape, F32),
            jax.ShapeDtypeStruct(tip_right.shape, F32),
        ),
        in_specs=[vmem] * 7,
        out_specs=(vmem, vmem),
        scratch_shapes=[
            pltpu.VMEM((2, n, n), F32),
            pltpu.VMEM((2, n, wide), F32),
            pltpu.VMEM((k, wide), F32),
            pltpu.VMEM((n, n), F32),
            pltpu.VMEM((n, wide), F32),
            pltpu.VMEM((levels + 1, 2, n, n), F32),
            pltpu.VMEM((2, n, n), F32),
            pltpu.VMEM((levels + 2, n, wide), F32),
            pltpu.VMEM((levels, n, n), F32),
            pltpu.VMEM((levels, n, wide), F32),
            pltpu.VMEM((levels, n, n), F32),
            pltpu.VMEM((levels, n, wide), F32),
            pltpu.VMEM((levels, k, wide), F32),
            pltpu.VMEM((levels + 1, 2, n, m), F32),
            pltpu.VMEM((k, m), F32),
            pltpu.SemaphoreType.DMA((6,)),
            pltpu.SemaphoreType.DMA((levels, 6)),
            pltpu.SemaphoreType.DMA((levels, 3)),
            pltpu.SemaphoreType.DMA((3,)),
        ],
        compiler_params=pltpu.CompilerParams(
            collective_id=0, has_side_effects=True, vmem_limit_bytes=67000000
        ),
        name="arrow_solve",
    )(transition, innovation, observation, effects, prior.reshape(1, k), right_side, tip_right)


def solution(mesh):
    placed = (
        P(AXES, None, None),
        P(AXES, None),
        P(AXES, None),
        P(AXES, None, None),
        P(),
        P(AXES, None, None),
        P(),
    )
    return jax.shard_map(
        body,
        mesh=mesh,
        in_specs=placed,
        out_specs=(P(AXES, None, None), P()),
        check_vma=False,
    )
```

time: 671 us -> 351 us (0.52); the launches traced: 658 us -> 351 us
  starting transfers between devices: 200 us -> 0 us
  matrix products: 165 us -> 0 us
  Pallas kernels: 192 us -> 346 us
  waiting for transfers between devices: 62.1 us -> 0 us
  other arithmetic: 29.8 us -> 0 us
    ppermute x68 -> x0, starting transfers between devices: 200 us -> none  [send(): return lax.ppermute(values, AXES, pairs)]
    dot_general x106 -> x0, matrix products: 165 us -> none  [the longest x56 94.9 us: gram_prod(): return jnp.einsum('ji,jk->ik', left, right, precision=precision)]
    pallas_call x8 -> x1, Pallas kernels: 192 us -> 346 us  [body(): pl.pallas_call(functools.partial(kernel, levels, shorts), out_shape=(jax....]
    ppermute x68 -> x0, waiting for transfers between devices: 62.1 us -> none  [send(): return lax.ppermute(values, AXES, pairs)]
    sub x12 -> x0, other arithmetic: 14.8 us -> none  [the longest x5 7.32 us: body(): node_arrow = node_arrow - arrow_right - arrow_left]
    add x14 -> x0, other arithmetic: 10.8 us -> none  [the longest x5 4.55 us: body(): tip_solution = tip_solution + send(tip_solution, back_right)]
  transfers between devices with their start and end apart: 68 -> 0, of which waited for: 10 -> 0; matrix products, arithmetic and copies ran while one was open for 27% -> 0% of each run, Pallas kernels for 26% -> 0%
where the time goes in v1:
time: 351 us
  Pallas kernels  346 us (99%)
  local copies, waits for them, and re-layouts  4.63 us (1%)
    pallas_call x1, Pallas kernels, body(): pl.pallas_call(functools.partial(kernel, levels, shorts), out_shape=(jax....  346 us

profile of v1, /device:TPU:15, one launch (start us, length us, event | category | flops | bytes accessed | tf_op | source)
XLA Modules:
  0.0 351.1 jit_solution(3935436457674487388)
XLA Ops:
  0.6 1.2 reshape.7.prior
  1.9 345.8 %arrow_solve.1 = (f32[2,384,128]{2,1,0:T(8,128)}, f32[384,128]{1,0:T(8,128)}) custom-call(f32[2,384,384]{2,1,0:T(8,128)} %trans.1, f32[2,384]{1,0:T(2,128)} %innov.1, f32[2,384]{1,0:T(2,128)} %observ.1, f32[2,384,384]{2,1,0:T(8,128)} %effects.1, f32[1,384]{1,0:T(1,128)} %reshape.7.prior, f32[2,384,128]{2,1,0:T(8,128)} %right.1, f32[384,128]{1,0:T(8,128)} %tip_right.1), custom_call_target="tpu_custom_call" | custom-call | tf_op jit(solution)/shard_map/arrow_solve/pallas_call | solution.py:409
  347.7 1.8 copy.11
  349.5 1.6 copy.12
